TPU v7x, 512 devices: a whole 4x8x8 slice. The times are simulated.
512 devices in a mesh: seq: 64 (over z_hi, y, core), head: 8 (over x, z_lo).
Axes of the slice: x: 4, y: 8, z: 8 (z_hi: 4, z_lo: 2; z = z_hi * 2 + z_lo), core: 2. Of those that a mesh axis runs over, the one named last changes fastest.
Arguments:
- target: bfloat16 [16384, 2048], P('seq', 'head'), may hold values from -1000 to 1000, as said below
- source: bfloat16 [16384, 2048], P('seq', 'head'), may hold values from -6 to 6
- w_query: bfloat16 [2048, 2048], P('seq', 'head'), may hold values from -0.125 to 0.125
- w_key: bfloat16 [2048, 2048], P('seq', 'head'), may hold values from -0.125 to 0.125
- w_value: bfloat16 [2048, 2048], P('seq', 'head'), may hold values from -0.125 to 0.125
- w_out: bfloat16 [2048, 2048], P('seq', 'head'), may hold values from -0.125 to 0.125
- band_start: int32 [256], P('seq'), may hold values from 0 to 255, as said below
- band_end: int32 [256], P('seq'), may hold values from 1 to 256, as said below
- cotangent: bfloat16 [16384, 2048], P('seq', 'head'), may hold values from -6 to 6
Outputs:
- attended: bfloat16 [16384, 2048], P('seq', 'head')
- grad_target: bfloat16 [16384, 2048], P('seq', 'head')
- grad_source: bfloat16 [16384, 2048], P('seq', 'head')
Inputs may be any that keep to these rules, and one draw needn't show every extreme that they name: `target`: activations of order one, at most some rows much larger. band_start and band_end never fall from block to block; band_start[b] >= b - 1, band_start[b] < band_end[b] <= band_start[b] + 3, band_end[b] <= b + 3; some target block has a band of exactly 3 source blocks. `band_end`: see band_start.
All inputs are finite; a program needn't handle non-finite values.
Results may differ from a plain program's by a relative error of at most 0.02.
Values may be sent and summed in bfloat16 or wider, within the bound.
No kernel may reach another device: no remote copies, remote signals or barrier semaphores. Data moves between devices by JAX's collectives and lax.ppermute only.
A program may use at most 64 MiB of HBM per device.

v0:
```python
import jax
import jax.numpy as jnp
from jax import lax
from jax.sharding import PartitionSpec as P

HEAD_DIM = 128
BLOCK = 64
MAXW = 3


def passed_along(shard, axis, by):
    count = lax.axis_size(axis)
    pairs = [(i, i + by) for i in range(count) if 0 <= i + by < count]
    return lax.ppermute(shard, axis, pairs)


def fold_rows(weight, piece):
    return jnp.dot(piece, weight, preferred_element_type=jnp.float32)


def times_transpose(left, right):
    return lax.dot_general(
        left, right, (((1,), (1,)), ((), ())), preferred_element_type=jnp.float32
    )


def per_device(target, source, w_query, w_key, w_value, w_out, band_start, band_end, cotangent):
    fone = jnp.float32
    half = jnp.bfloat16
    rows = target.shape[0]
    width = w_query.shape[1]
    heads = width // HEAD_DIM
    blocks = rows // BLOCK
    right_rows = (MAXW - 1) * BLOCK
    scale = HEAD_DIM ** (-0.5)
    wq, wk, wv, wo = (
        lax.all_gather(w_query, "seq", axis=0, tiled=True),
        lax.all_gather(w_key, "seq", axis=0, tiled=True),
        lax.all_gather(w_value, "seq", axis=0, tiled=True),
        lax.all_gather(w_out, "seq", axis=0, tiled=True),
    )
    query = fold_rows(wq, lax.all_gather(target, "head", axis=1, tiled=True)).astype(half)
    piece = lax.all_gather(source, "head", axis=1, tiled=True)
    key_sum = fold_rows(wk, piece)
    value_sum = fold_rows(wv, piece)
    packed = jnp.concatenate([key_sum.astype(half), value_sum.astype(half)], 1)
    from_prev = passed_along(packed[rows - BLOCK :], "seq", 1)
    from_next = passed_along(packed[:right_rows], "seq", -1)
    window = jnp.concatenate([from_prev, packed, from_next], 0)
    span_all = window.shape[0]
    anchor = lax.axis_index("seq") * blocks - 1
    low = band_start - anchor
    high = band_end - anchor
    count = 1
    q_blocks = query.reshape(1, rows, heads, HEAD_DIM)
    kv_blocks = window.reshape(1, span_all, 2 * heads, HEAD_DIM)
    key_block = (jnp.arange(span_all, dtype=jnp.int32) // BLOCK)[None, :]
    low_rows = jnp.repeat(low, BLOCK)[None, :]
    high_rows = jnp.repeat(high, BLOCK)[None, :]
    k_blocks = kv_blocks[:, :, :heads]
    v_blocks = kv_blocks[:, :, heads:]
    visible = (key_block[:, None, :] >= low_rows[:, :, None]) & (
        key_block[:, None, :] < high_rows[:, :, None]
    )
    scores = jnp.einsum("nqhe,nkhe->nhqk", q_blocks, k_blocks, preferred_element_type=fone) * scale
    scores = jnp.where(visible[:, None], scores, -jnp.inf)
    top = jnp.max(scores, axis=-1, keepdims=True)
    expo = jnp.exp(scores - top)
    prob = expo / jnp.sum(expo, axis=-1, keepdims=True)
    prob_b = prob.astype(half)
    context = jnp.einsum("nhqk,nkhe->nqhe", prob_b, v_blocks, preferred_element_type=fone).astype(
        half
    )
    context_flat = context.reshape(rows, width)
    attended = (
        lax.psum_scatter(
            times_transpose(context_flat, wo).astype(jnp.bfloat16),
            "head",
            scatter_dimension=1,
            tiled=True,
        )
        .astype(jnp.float32)
        .astype(half)
    )
    d_context = fold_rows(wo, lax.all_gather(cotangent, "head", axis=1, tiled=True)).astype(half)
    dc_blocks = d_context.reshape(context.shape)
    delta = jnp.sum(dc_blocks.astype(fone) * context.astype(fone), axis=-1)
    delta = jnp.transpose(delta, (0, 2, 1))[..., None]
    d_prob = jnp.einsum("nqhe,nkhe->nhqk", dc_blocks, v_blocks, preferred_element_type=fone)
    d_score = (prob * (d_prob - delta) * scale).astype(half)
    d_query = jnp.einsum("nhqk,nkhe->nqhe", d_score, k_blocks, preferred_element_type=fone).astype(
        half
    )
    dk_blocks = jnp.einsum("nhqk,nqhe->nkhe", d_score, q_blocks, preferred_element_type=fone)
    dv_blocks = jnp.einsum("nhqk,nqhe->nkhe", prob_b, dc_blocks, preferred_element_type=fone)
    dkv_blocks = jnp.concatenate(
        [dk_blocks.reshape(count, span_all, width), dv_blocks.reshape(count, span_all, width)], 2
    )
    dkv_window = dkv_blocks.reshape(span_all, 2 * width)
    back_next = passed_along(dkv_window[:BLOCK], "seq", -1)
    back_prev = passed_along(dkv_window[BLOCK + rows :], "seq", 1)
    owned = dkv_window[BLOCK : BLOCK + rows]
    owned = owned.at[rows - BLOCK :].add(back_next)
    owned = owned.at[:right_rows].add(back_prev)
    d_key = owned[:, :width].astype(half)
    d_value = owned[:, width:].astype(half)
    d_query_flat = d_query.reshape(rows, width)
    grad_target = (
        lax.psum_scatter(
            times_transpose(d_query_flat, wq).astype(jnp.bfloat16),
            "head",
            scatter_dimension=1,
            tiled=True,
        )
        .astype(jnp.float32)
        .astype(half)
    )
    source_term = times_transpose(d_key, wk) + times_transpose(d_value, wv)
    grad_source = (
        lax.psum_scatter(source_term.astype(jnp.bfloat16), "head", scatter_dimension=1, tiled=True)
        .astype(jnp.float32)
        .astype(half)
    )
    return (attended, grad_target, grad_source)


def solution(mesh):
    in_specs = (
        P("seq", "head"),
        P("seq", "head"),
        P("seq", "head"),
        P("seq", "head"),
        P("seq", "head"),
        P("seq", "head"),
        P("seq"),
        P("seq"),
        P("seq", "head"),
    )
    out_specs = (P("seq", "head"), P("seq", "head"), P("seq", "head"))
    return jax.shard_map(
        per_device, mesh=mesh, in_specs=in_specs, out_specs=out_specs, check_vma=False
    )
```

profile of v0, /device:TPU:8, one launch (start us, length us, event | category | flops | bytes accessed | tf_op | source)
XLA Modules:
  0.0 650.5 jit_solution(3358592871795059263)
XLA Ops:
  7.2 0.7 all-gather.8.cloned.1.call-update
  7.9 0.7 all-gather.12.cloned.1.call-update
  8.7 0.7 all-gather.10.cloned.1.call-update
  10.0 0.5 all-gather.16.cloned.1.call-update
  11.2 0.7 all-gather.18.cloned.1.call-update
  11.9 0.7 broadcast_subtract_fusion
  13.1 46.8 %all-gather.8.cloned.1.call-done = bf16[256,2048]{1,0:T(8,128)(2,1)} async-done(((bf16[256,256]{1,0:T(8,128)(2,1)}), bf16[256,2048]{1,0:T(8,128)(2,1)}) %all-gather.8.cloned.1.call-update) | async-done | bytes 1048592 | tf_op jit(solution)/shard_map/all_gather | solution.py:43
  59.9 86.9 %all-gather.12.cloned.1.call-done = bf16[2048,256]{1,0:T(8,128)(2,1)} async-done(((bf16[32,256]{1,0:T(8,128)(2,1)}), bf16[2048,256]{1,0:T(8,128)(2,1)}) %all-gather.12.cloned.1.call-update) | async-done | bytes 1048592 | tf_op jit(solution)/shard_map/all_gather | solution.py:39
  146.8 2.1 convolution_convert_fusion.6
  148.9 81.7 %all-gather.10.cloned.1.call-done = bf16[2048,256]{1,0:T(8,128)(2,1)} async-done(((bf16[32,256]{1,0:T(8,128)(2,1)}), bf16[2048,256]{1,0:T(8,128)(2,1)}) %all-gather.10.cloned.1.call-update) | async-done | bytes 1048592 | tf_op jit(solution)/shard_map/all_gather | solution.py:38
  230.6 1.7 convolution_convert_fusion.7
  232.4 2.1 collective-permute-start
  234.6 3.4 collective-permute-start.1
  238.0 37.7 %all-gather.14.cloned.1.call-done = bf16[256,2048]{1,0:T(8,128)(2,1)} async-done(((bf16[256,256]{1,0:T(8,128)(2,1)}), bf16[256,2048]{1,0:T(8,128)(2,1)}) %all-gather.14.cloned.1.call-update) | async-done | bytes 1048592 | tf_op jit(solution)/shard_map/all_gather | solution.py:42
  275.7 86.8 %all-gather.16.cloned.1.call-done = bf16[2048,256]{1,0:T(8,128)(2,1)} async-done(((bf16[32,256]{1,0:T(8,128)(2,1)}), bf16[2048,256]{1,0:T(8,128)(2,1)}) %all-gather.16.cloned.1.call-update) | async-done | bytes 1048592 | tf_op jit(solution)/shard_map/all_gather | solution.py:37
  362.5 2.1 convolution_convert_fusion.5
  364.6 43.1 %all-gather.20.cloned.1.call-done = bf16[256,2048]{1,0:T(8,128)(2,1)} async-done(((bf16[256,256]{1,0:T(8,128)(2,1)}), bf16[256,2048]{1,0:T(8,128)(2,1)}) %all-gather.20.cloned.1.call-update) | async-done | bytes 1048592 | tf_op jit(solution)/shard_map/all_gather | solution.py:85
  407.7 86.9 %all-gather.18.cloned.1.call-done = bf16[2048,256]{1,0:T(8,128)(2,1)} async-done(((bf16[32,256]{1,0:T(8,128)(2,1)}), bf16[2048,256]{1,0:T(8,128)(2,1)}) %all-gather.18.cloned.1.call-update) | async-done | bytes 1048592 | tf_op jit(solution)/shard_map/all_gather | solution.py:40
  494.6 2.1 convolution_convert_fusion.4
  497.5 0.7 fusion.10
  498.7 1.5 convolution_convert_fusion.1
  500.8 0.7 copy-done.1
  501.5 1.5 convolution_convert_fusion
  503.7 0.7 convolution_bitcast_fusion
  505.0 3.1 collective-permute-start.2
  508.4 2.1 collective-permute-start.3
  511.0 5.2 collective-permute-done.3
  516.8 0.7 copy-done.4
  517.5 1.4 fusion.1
  519.0 26.4 %reduce-scatter.4.cloned.1.call-done = bf16[256,256]{1,0:T(8,128)(2,1)} async-done(((bf16[256,2048]{1,0:T(8,128)(2,1)}), bf16[256,256]{1,0:T(8,128)(2,1)}) %reduce-scatter.4.cloned.1.call-update) | async-done | bytes 131088 | tf_op jit(solution)/shard_map/reduce_scatter | solution.py:76
  545.4 49.6 %reduce-scatter.6.cloned.1.call-done = bf16[256,256]{1,0:T(8,128)(2,1)} async-done(((bf16[256,2048]{1,0:T(8,128)(2,1)}), bf16[256,256]{1,0:T(8,128)(2,1)}) %reduce-scatter.6.cloned.1.call-update) | async-done | bytes 131088 | tf_op jit(solution)/shard_map/reduce_scatter | solution.py:109
  595.1 48.6 %reduce-scatter.8.cloned.1.call-done = bf16[256,256]{1,0:T(8,128)(2,1)} async-done(((bf16[256,2048]{1,0:T(8,128)(2,1)}), bf16[256,256]{1,0:T(8,128)(2,1)}) %reduce-scatter.8.cloned.1.call-update) | async-done | bytes 131088 | tf_op jit(solution)/shard_map/reduce_scatter | solution.py:120
  (51 shorter events, 6.5 us)
Async XLA Ops:
  7.2 52.8 %all-gather.8.cloned.1.call-start = ((), (), s32[]{:S(2)}) async-start(), calls=%async_computation.3 | async-start | bytes 1179648 | tf_op jit(solution)/shard_map/all_gather | solution.py:43
  7.9 138.9 %all-gather.12.cloned.1.call-start = ((), (), s32[]{:S(2)}) async-start(), calls=%async_computation.5 | async-start | bytes 1064960 | tf_op jit(solution)/shard_map/all_gather | solution.py:39
  8.6 221.9 %all-gather.10.cloned.1.call-start = ((), (), s32[]{:S(2)}) async-start(), calls=%async_computation.4 | async-start | bytes 1064960 | tf_op jit(solution)/shard_map/all_gather | solution.py:38
  9.4 266.4 %all-gather.14.cloned.1.call-start = ((), (), s32[]{:S(2)}) async-start(), calls=%async_computation.6 | async-start | bytes 1179648 | tf_op jit(solution)/shard_map/all_gather | solution.py:42
  10.0 352.6 %all-gather.16.cloned.1.call-start = ((), (), s32[]{:S(2)}) async-start(), calls=%async_computation.7 | async-start | bytes 1064960 | tf_op jit(solution)/shard_map/all_gather | solution.py:37
  10.5 397.1 %all-gather.20.cloned.1.call-start = ((), (), s32[]{:S(2)}) async-start(), calls=%async_computation.10 | async-start | bytes 1179648 | tf_op jit(solution)/shard_map/all_gather | solution.py:85
  11.1 483.5 %all-gather.18.cloned.1.call-start = ((), (), s32[]{:S(2)}) async-start(), calls=%async_computation.8 | async-start | bytes 1064960 | tf_op jit(solution)/shard_map/all_gather | solution.py:40
  11.9 533.6 %reduce-scatter.4.cloned.1.call-start = ((), (), s32[]{:S(2)}) async-start(), calls=%async_computation.9 | async-start | bytes 1179648 | tf_op jit(solution)/shard_map/reduce_scatter | solution.py:76
  59.9 170.7 %copy-start.2 = (bf16[256,2048]{1,0:T(8,128)(2,1)S(1)}, bf16[256,2048]{1,0:T(8,128)(2,1)}, u32[]{:S(2)}) copy-start(bf16[256,2048]{1,0:T(8,128)(2,1)} %all-gather.8.cloned.1.call-done) | copy-start | bytes 3145732
  232.4 264.3 %collective-permute-start = (bf16[64,512]{0,1:T(8,128)(2,1)S(1)}, bf16[64,512]{0,1:T(8,128)(2,1)S(1)}, u32[]{:S(2)}, u32[]{:S(2)}) collective-permute-start(bf16[64,512]{0,1:T(8,128)(2,1)S(1)} %fusion.13), channel_id=1, source_target_pairs={{0,8},{8,16},{16,24},{24,32},{32,40},{40,48},{48,56},{56,64},{64,7... | collective-permute-start | bytes 196616 | tf_op jit(solution)/shard_map/ppermute | solution.py:14
  234.6 262.1 %collective-permute-start.1 = (bf16[128,512]{0,1:T(8,128)(2,1)S(1)}, bf16[128,512]{0,1:T(8,128)(2,1)S(1)}, u32[]{:S(2)}, u32[]{:S(2)}) collective-permute-start(bf16[128,512]{0,1:T(8,128)(2,1)S(1)} %pad_maximum_fusion.2), channel_id=1, source_target_pairs={{8,0},{16,8},{24,16},{32,24},{40,32},{48,40},{56,48},{64,56},{72,6... | collective-permute-start | bytes 393224 | tf_op jit(solution)/shard_map/ppermute | solution.py:14
  497.5 1.2 copy-start.3
  500.2 94.9 %reduce-scatter.6.cloned.1.call-start = ((), (), s32[]{:S(2)}) async-start(), calls=%async_computation.11 | async-start | bytes 1179648 | tf_op jit(solution)/shard_map/reduce_scatter | solution.py:109
  500.3 1.2 copy-start.1
  503.0 140.7 %reduce-scatter.8.cloned.1.call-start = ((), (), s32[]{:S(2)}) async-start(), calls=%async_computation.12 | async-start | bytes 1179648 | tf_op jit(solution)/shard_map/reduce_scatter | solution.py:120
  505.0 6.0 collective-permute-start.2
  508.4 8.0 %copy-start = (bf16[2048,256]{1,0:T(8,128)(2,1)S(1)}, bf16[2048,256]{1,0:T(8,128)(2,1)}, u32[]{:S(2)}) copy-start(bf16[2048,256]{1,0:T(8,128)(2,1)} %all-gather.12.cloned.1.call-done) | copy-start | bytes 3145732
  508.4 7.8 %collective-permute-start.3 = (f32[128,512]{1,0:T(8,128)S(1)}, f32[128,512]{1,0:T(8,128)S(1)}, u32[]{:S(2)}, u32[]{:S(2)}) collective-permute-start(f32[128,512]{1,0:T(8,128)S(1)} %bitcast.115), channel_id=1, source_target_pairs={{0,8},{8,16},{16,24},{24,32},{32,40},{40,48},{48,56},{56,64},{64,7... | collective-permute-start | bytes 786440 | tf_op jit(solution)/shard_map/ppermute | solution.py:14
  516.3 1.2 copy-start.4
Sparse Core Ops, SparseCore 0:
  10.0 49.8 all-gather.7
  63.3 83.5 all-gather.11
  150.2 80.3 all-gather.9
  232.4 43.2 all-gather.13
  279.0 83.5 all-gather.15
  364.4 43.2 all-gather.19
  411.1 83.5 all-gather.17
  500.3 45.0 reduce-scatter.3
  548.8 46.1 reduce-scatter.5
  598.3 45.2 reduce-scatter.7
where the time goes:
time: 651 us; the launch traced here: 650 us
  waiting for transfers between devices  604 us (93%)
  matrix products  15.5 us (2%)
  between operations  14.4 us (2%)
  starting transfers between devices  11.1 us (2%)
    all_gather x1, waiting for transfers between devices, per_device(): lax.all_gather(w_out, 'seq', axis=0, tiled=True)  86.9 us
    all_gather x1, waiting for transfers between devices, per_device(): lax.all_gather(w_value, 'seq', axis=0, tiled=True)  86.9 us
    all_gather x1, waiting for transfers between devices, per_device(): lax.all_gather(w_query, 'seq', axis=0, tiled=True)  86.8 us
    all_gather x1, waiting for transfers between devices, per_device(): lax.all_gather(w_key, 'seq', axis=0, tiled=True)  81.7 us
    reduce_scatter x1, waiting for transfers between devices, per_device(): lax.psum_scatter(times_transpose(d_query_flat, wq).astype(jnp.bfloat16),...  49.6 us
    reduce_scatter x1, waiting for transfers between devices, per_device(): lax.psum_scatter(source_term.astype(jnp.bfloat16), 'head', scatter_dimens...  48.6 us
    all_gather x1, waiting for transfers between devices, per_device(): piece = lax.all_gather(source, 'head', axis=1, tiled=True)  46.8 us
    all_gather x1, waiting for transfers between devices, per_device(): lax.all_gather(cotangent, 'head', axis=1, tiled=True)  43.1 us
  transfers between devices with their start and end apart: 14, of which 11 were waited for; matrix products, arithmetic and copies ran while one was open for 2% of the time, Pallas kernels for 0%

commit v1 on v0

--- a/solution.py
+++ b/solution.py
@@ -35,7 +35,9 @@
     scale = HEAD_DIM ** (-0.5)
     wq, wk, wv, wo = (
         lax.all_gather(w_query, "seq", axis=0, tiled=True),
-        lax.all_gather(w_key, "seq", axis=0, tiled=True),
+        jnp.concatenate(
+            lax.all_to_all(jnp.stack([w_key] * lax.axis_size("seq")), "seq", 0, 0), axis=0
+        ),
         lax.all_gather(w_value, "seq", axis=0, tiled=True),
         lax.all_gather(w_out, "seq", axis=0, tiled=True),
     )

time: 651 us -> 589 us (0.905)
  waiting for transfers between devices: 604 us -> 526 us
  starting transfers between devices: 11.1 us -> 27.7 us
    all_gather x1 -> x0, waiting for transfers between devices: 81.7 us -> none  [per_device(): lax.all_gather(w_key, 'seq', axis=0, tiled=True)]
    all_to_all x0 -> x1, starting transfers between devices: none -> 16.6 us  [per_device(): lax.all_to_all(jnp.stack([w_key] * lax.axis_size('seq')), 'seq', 0, 0)]
  transfers between devices with their start and end apart: 14 -> 14, of which waited for: 11 -> 10; matrix products, arithmetic and copies ran while one was open for 2% -> 3% of each run, Pallas kernels for 0% -> 0%
where the time goes in v1:
time: 589 us
  waiting for transfers between devices  526 us (89%)
  starting transfers between devices  27.7 us (5%)
  matrix products  16.4 us (3%)
  between operations  14.2 us (2%)
    all_gather x1, waiting for transfers between devices, per_device(): lax.all_gather(w_value, 'seq', axis=0, tiled=True)  87.2 us
    all_gather x1, waiting for transfers between devices, per_device(): lax.all_gather(w_out, 'seq', axis=0, tiled=True)  86.8 us
    all_gather x1, waiting for transfers between devices, per_device(): lax.all_gather(w_query, 'seq', axis=0, tiled=True)  86.8 us
    all_gather x1, waiting for transfers between devices, per_device(): piece = lax.all_gather(source, 'head', axis=1, tiled=True)  51.1 us
    reduce_scatter x1, waiting for transfers between devices, per_device(): lax.psum_scatter(times_transpose(d_query_flat, wq).astype(jnp.bfloat16),...  49.4 us
    reduce_scatter x1, waiting for transfers between devices, per_device(): lax.psum_scatter(source_term.astype(jnp.bfloat16), 'head', scatter_dimens...  48.8 us
    all_gather x1, waiting for transfers between devices, per_device(): lax.all_gather(cotangent, 'head', axis=1, tiled=True)  43.1 us
    all_gather x1, waiting for transfers between devices, per_device(): lax.all_gather(target, 'head', axis=1, tiled=True)  37 us
  transfers between devices with their start and end apart: 14, of which 10 were waited for; matrix products, arithmetic and copies ran while one was open for 3% of the time, Pallas kernels for 0%

profile of v1, /device:TPU:8, one launch (start us, length us, event | category | flops | bytes accessed | tf_op | source)
XLA Modules:
  0.0 588.9 jit_solution(7841244516481361144)
XLA Ops:
  7.2 0.7 all-gather.7.cloned.1.call-update
  8.0 0.7 all-gather.9.cloned.1.call-update
  8.7 0.7 all-gather.11.cloned.1.call-update
  9.4 0.5 all-gather.13.cloned.1.call-update
  10.0 0.5 all-gather.17.cloned.1.call-update
  10.6 1.8 stack.2
  12.4 16.6 %all-to-all-start = ((bf16[64,32,256]{2,1,0:T(8,128)(2,1)}), bf16[64,32,256]{2,1,0:T(8,128)(2,1)S(1)}, u32[]{:S(2)}, u32[]{:S(2)}) async-start(bf16[64,32,256]{2,1,0:T(8,128)(2,1)} %stack.2), calls=%async_computation | async-start | bytes 2097152 | tf_op jit(solution)/shard_map/all_to_all | solution.py:39
  29.0 0.5 all-gather.15.cloned.1.call-update
  30.1 51.1 %all-gather.7.cloned.1.call-done = bf16[256,2048]{1,0:T(8,128)(2,1)} async-done(((bf16[256,256]{1,0:T(8,128)(2,1)}), bf16[256,2048]{1,0:T(8,128)(2,1)}) %all-gather.7.cloned.1.call-update) | async-done | bytes 1048592 | tf_op jit(solution)/shard_map/all_gather | solution.py:45
  81.2 87.2 %all-gather.9.cloned.1.call-done = bf16[2048,256]{1,0:T(8,128)(2,1)} async-done(((bf16[32,256]{1,0:T(8,128)(2,1)}), bf16[2048,256]{1,0:T(8,128)(2,1)}) %all-gather.9.cloned.1.call-update) | async-done | bytes 1048592 | tf_op jit(solution)/shard_map/all_gather | solution.py:41
  168.5 2.1 convolution_convert_fusion.6
  171.2 2.1 collective-permute-start
  173.3 3.4 collective-permute-start.1
  176.8 37.0 %all-gather.11.cloned.1.call-done = bf16[256,2048]{1,0:T(8,128)(2,1)} async-done(((bf16[256,256]{1,0:T(8,128)(2,1)}), bf16[256,2048]{1,0:T(8,128)(2,1)}) %all-gather.11.cloned.1.call-update) | async-done | bytes 1048592 | tf_op jit(solution)/shard_map/all_gather | solution.py:44
  213.8 86.8 %all-gather.13.cloned.1.call-done = bf16[2048,256]{1,0:T(8,128)(2,1)} async-done(((bf16[32,256]{1,0:T(8,128)(2,1)}), bf16[2048,256]{1,0:T(8,128)(2,1)}) %all-gather.13.cloned.1.call-update) | async-done | bytes 1048592 | tf_op jit(solution)/shard_map/all_gather | solution.py:37
  300.6 2.1 convolution_convert_fusion.5
  302.6 43.1 %all-gather.17.cloned.1.call-done = bf16[256,2048]{1,0:T(8,128)(2,1)} async-done(((bf16[256,256]{1,0:T(8,128)(2,1)}), bf16[256,2048]{1,0:T(8,128)(2,1)}) %all-gather.17.cloned.1.call-update) | async-done | bytes 1048592 | tf_op jit(solution)/shard_map/all_gather | solution.py:87
  345.7 86.8 %all-gather.15.cloned.1.call-done = bf16[2048,256]{1,0:T(8,128)(2,1)} async-done(((bf16[32,256]{1,0:T(8,128)(2,1)}), bf16[2048,256]{1,0:T(8,128)(2,1)}) %all-gather.15.cloned.1.call-update) | async-done | bytes 1048592 | tf_op jit(solution)/shard_map/all_gather | solution.py:42
  432.5 2.1 convolution_convert_fusion.4
  434.9 1.4 fusion.27
  436.3 0.7 fusion.10
  437.5 1.5 convolution_convert_fusion.1
  439.0 1.6 fusion.7
  440.9 1.5 convolution_convert_fusion
  443.1 0.7 convolution_bitcast_fusion
  444.4 3.1 collective-permute-start.2
  447.8 2.1 collective-permute-start.3
  450.4 5.2 collective-permute-done.3
  456.2 1.5 fusion.1
  457.7 26.5 %reduce-scatter.4.cloned.1.call-done = bf16[256,256]{1,0:T(8,128)(2,1)} async-done(((bf16[256,2048]{1,0:T(8,128)(2,1)}), bf16[256,256]{1,0:T(8,128)(2,1)}) %reduce-scatter.4.cloned.1.call-update) | async-done | bytes 131088 | tf_op jit(solution)/shard_map/reduce_scatter | solution.py:78
  484.2 49.4 %reduce-scatter.6.cloned.1.call-done = bf16[256,256]{1,0:T(8,128)(2,1)} async-done(((bf16[256,2048]{1,0:T(8,128)(2,1)}), bf16[256,256]{1,0:T(8,128)(2,1)}) %reduce-scatter.6.cloned.1.call-update) | async-done | bytes 131088 | tf_op jit(solution)/shard_map/reduce_scatter | solution.py:111
  533.6 48.8 %reduce-scatter.8.cloned.1.call-done = bf16[256,256]{1,0:T(8,128)(2,1)} async-done(((bf16[256,2048]{1,0:T(8,128)(2,1)}), bf16[256,256]{1,0:T(8,128)(2,1)}) %reduce-scatter.8.cloned.1.call-update) | async-done | bytes 131088 | tf_op jit(solution)/shard_map/reduce_scatter | solution.py:122
  (53 shorter events, 5.1 us)
Async XLA Ops:
  7.2 22.4 %copy-start.4 = (s32[4]{0:T(128)S(1)}, s32[4]{0:T(128)}, u32[]{:S(2)}) copy-start(s32[4]{0:T(128)} %param.20) | copy-start | bytes 52
  7.2 22.4 %copy-start.5 = (s32[4]{0:T(128)S(1)}, s32[4]{0:T(128)}, u32[]{:S(2)}) copy-start(s32[4]{0:T(128)} %param.19) | copy-start | bytes 52
  7.2 74.0 %all-gather.7.cloned.1.call-start = ((), (), s32[]{:S(2)}) async-start(), calls=%async_computation.4 | async-start | bytes 1179648 | tf_op jit(solution)/shard_map/all_gather | solution.py:45
  7.9 160.5 %all-gather.9.cloned.1.call-start = ((), (), s32[]{:S(2)}) async-start(), calls=%async_computation.5 | async-start | bytes 1064960 | tf_op jit(solution)/shard_map/all_gather | solution.py:41
  8.7 205.1 %all-gather.11.cloned.1.call-start = ((), (), s32[]{:S(2)}) async-start(), calls=%async_computation.6 | async-start | bytes 1179648 | tf_op jit(solution)/shard_map/all_gather | solution.py:44
  9.4 291.2 %all-gather.13.cloned.1.call-start = ((), (), s32[]{:S(2)}) async-start(), calls=%async_computation.7 | async-start | bytes 1064960 | tf_op jit(solution)/shard_map/all_gather | solution.py:37
  10.0 335.7 %all-gather.17.cloned.1.call-start = ((), (), s32[]{:S(2)}) async-start(), calls=%async_computation.10 | async-start | bytes 1179648 | tf_op jit(solution)/shard_map/all_gather | solution.py:87
  12.4 158.1 %all-to-all-start = ((bf16[64,32,256]{2,1,0:T(8,128)(2,1)}), bf16[64,32,256]{2,1,0:T(8,128)(2,1)S(1)}, u32[]{:S(2)}, u32[]{:S(2)}) async-start(bf16[64,32,256]{2,1,0:T(8,128)(2,1)} %stack.2), calls=%async_computation | async-start | bytes 2097152 | tf_op jit(solution)/shard_map/all_to_all | solution.py:39
  29.0 403.5 %all-gather.15.cloned.1.call-start = ((), (), s32[]{:S(2)}) async-start(), calls=%async_computation.8 | async-start | bytes 1064960 | tf_op jit(solution)/shard_map/all_gather | solution.py:42
  29.5 454.7 %reduce-scatter.4.cloned.1.call-start = ((), (), s32[]{:S(2)}) async-start(), calls=%async_computation.9 | async-start | bytes 1179648 | tf_op jit(solution)/shard_map/reduce_scatter | solution.py:78
  81.2 89.3 %copy-start.3 = (bf16[256,2048]{1,0:T(8,128)(2,1)S(1)}, bf16[256,2048]{1,0:T(8,128)(2,1)}, u32[]{:S(2)}) copy-start(bf16[256,2048]{1,0:T(8,128)(2,1)} %all-gather.7.cloned.1.call-done) | copy-start | bytes 3145732
  171.2 263.4 %collective-permute-start = (bf16[64,512]{0,1:T(8,128)(2,1)S(1)}, bf16[64,512]{0,1:T(8,128)(2,1)S(1)}, u32[]{:S(2)}, u32[]{:S(2)}) collective-permute-start(bf16[64,512]{0,1:T(8,128)(2,1)S(1)} %fusion.13), channel_id=1, source_target_pairs={{0,8},{8,16},{16,24},{24,32},{32,40},{40,48},{48,56},{56,64},{64,7... | collective-permute-start | bytes 196616 | tf_op jit(solution)/shard_map/ppermute | solution.py:14
  173.3 261.2 %collective-permute-start.1 = (bf16[128,512]{0,1:T(8,128)(2,1)S(1)}, bf16[128,512]{0,1:T(8,128)(2,1)S(1)}, u32[]{:S(2)}, u32[]{:S(2)}) collective-permute-start(bf16[128,512]{0,1:T(8,128)(2,1)S(1)} %pad_maximum_fusion.2), channel_id=1, source_target_pairs={{8,0},{16,8},{24,16},{32,24},{40,32},{48,40},{56,48},{64,56},{72,6... | collective-permute-start | bytes 393224 | tf_op jit(solution)/shard_map/ppermute | solution.py:14
  436.3 1.2 copy-start.2
  439.0 94.6 %reduce-scatter.6.cloned.1.call-start = ((), (), s32[]{:S(2)}) async-start(), calls=%async_computation.11 | async-start | bytes 1179648 | tf_op jit(solution)/shard_map/reduce_scatter | solution.py:111
  439.0 1.8 copy-start.1
  442.4 140.0 %reduce-scatter.8.cloned.1.call-start = ((), (), s32[]{:S(2)}) async-start(), calls=%async_computation.12 | async-start | bytes 1179648 | tf_op jit(solution)/shard_map/reduce_scatter | solution.py:122
  444.4 6.0 %collective-permute-start.2 = (f32[64,512]{1,0:T(8,128)S(1)}, f32[64,512]{1,0:T(8,128)S(1)}, u32[]{:S(2)}, u32[]{:S(2)}) collective-permute-start(f32[64,512]{1,0:T(8,128)S(1)} %bitcast.123), channel_id=1, source_target_pairs={{8,0},{16,8},{24,16},{32,24},{40,32},{48,40},{56,48},{64,56},{72,6... | collective-permute-start | bytes 393224 | tf_op jit(solution)/shard_map/ppermute | solution.py:14
  447.8 8.0 %copy-start = (bf16[2048,256]{1,0:T(8,128)(2,1)S(1)}, bf16[2048,256]{1,0:T(8,128)(2,1)}, u32[]{:S(2)}) copy-start(bf16[2048,256]{1,0:T(8,128)(2,1)} %all-gather.9.cloned.1.call-done) | copy-start | bytes 3145732
  447.8 7.8 %collective-permute-start.3 = (f32[128,512]{1,0:T(8,128)S(1)}, f32[128,512]{1,0:T(8,128)S(1)}, u32[]{:S(2)}, u32[]{:S(2)}) collective-permute-start(f32[128,512]{1,0:T(8,128)S(1)} %bitcast.118), channel_id=1, source_target_pairs={{0,8},{8,16},{16,24},{24,32},{32,40},{40,48},{48,56},{56,64},{64,7... | collective-permute-start | bytes 786440 | tf_op jit(solution)/shard_map/ppermute | solution.py:14
Sparse Core Ops, SparseCore 0:
  10.0 71.1 all-gather.6
  84.6 83.8 all-gather.8
  170.5 43.2 all-gather.10
  217.0 83.5 all-gather.12
  302.4 43.2 all-gather.16
  348.9 83.5 all-gather.14
  439.1 45.0 reduce-scatter.3
  487.6 45.9 reduce-scatter.5
  537.0 45.3 reduce-scatter.7
